TPU v7x, 256 devices: a whole 4x4x8 slice. The times are simulated.
256 devices in a mesh: epoch: 16 (over x, y), row: 16 (over z, core).
Axes of the slice: x: 4, y: 4, z: 8, core: 2. Of those that a mesh axis runs over, the one named last changes fastest.
Arguments:
- forcing: float32 [16, 2, 128, 6144], P('epoch', None, 'row'), may hold values from -2400 to 2400
- observed: float32 [16, 2, 128, 6144], P('epoch', None, 'row'), may hold values from -6 to 6
- log_friction: float32 [128, 6144], P('row'), may hold values from -1.5 to 1.5
- log_rheology: float32 [128, 6144], P('row'), may hold values from -0.7 to 0.7
- grounded: int32 [128, 6144], P('row'), may hold values 0 or 1
Outputs:
- new_friction: float32 [128, 6144], P('row')
- new_rheology: float32 [128, 6144], P('row')
All inputs are finite; a program needn't handle non-finite values. No bound on the sum of `grounded` on one device may be relied on, other than what follows from the above.
Results may differ from a plain program's by a relative error of at most 0.00011.
Values sent between devices are 32-bit elements; how exact they have to be, the bound alone decides.
A program may use at most 64 MiB of HBM per device.

v0:
```python
import jax
import jax.numpy as jnp
from jax import lax
from jax.sharding import PartitionSpec as P

SWEEPS = 4
relax = 0.9
coupling = 0.1
step_size = 0.5


def padded(x, sides, width):
    for axis, dim in sides:
        devices, length = (lax.axis_size(axis), x.shape[dim])
        up = [(i, (i + 1) % devices) for i in range(devices - 1)]
        down = [(j, i) for i, j in up]
        last = lax.slice_in_dim(x, length - width, length, axis=dim)
        first = lax.slice_in_dim(x, 0, width, axis=dim)
        before = lax.ppermute(last, axis, up)
        after = lax.ppermute(first, axis, down)
        x = jnp.concatenate([before, x, after], axis=dim)
    return x


def shift_east(field):
    widths = [(0, 0)] * (field.ndim - 1) + [(0, 1)]
    return jnp.pad(field[..., 1:], widths)


def shift_west(field):
    widths = [(0, 0)] * (field.ndim - 1) + [(1, 0)]
    return jnp.pad(field[..., :-1], widths)


def cross_term(padded_comp):
    return (
        shift_east(padded_comp[2:])
        - shift_west(padded_comp[2:])
        - shift_east(padded_comp[:-2])
        + shift_west(padded_comp[:-2])
    )


def jacobi_sweep(padded_velocity, padded_stiffness, friction_coef, forcing_now):
    centre = padded_stiffness[1:-1]
    face_east = 0.5 * (centre + shift_east(centre))
    face_west = 0.5 * (centre + shift_west(centre))
    face_north = 0.5 * (centre + padded_stiffness[:-2])
    face_south = 0.5 * (centre + padded_stiffness[2:])
    along_sum = face_east + face_west
    across = face_north + face_south
    diag_u = 4.0 * along_sum + across + friction_coef + 0.5
    diag_v = along_sum + 4.0 * across + friction_coef + 0.5
    padded_u = padded_velocity[0]
    padded_v = padded_velocity[1]
    inner_u = padded_u[1:-1]
    inner_v = padded_v[1:-1]
    lateral_u = face_east * shift_east(inner_u) + face_west * shift_west(inner_u)
    vertical_u = face_north * padded_u[:-2] + face_south * padded_u[2:]
    lateral_v = face_east * shift_east(inner_v) + face_west * shift_west(inner_v)
    vertical_v = face_north * padded_v[:-2] + face_south * padded_v[2:]
    image_u = (
        diag_u * inner_u - 4.0 * lateral_u - vertical_u - coupling * centre * cross_term(padded_v)
    )
    image_v = (
        diag_v * inner_v - lateral_v - 4.0 * vertical_v - coupling * centre * cross_term(padded_u)
    )
    new_u = inner_u + relax * (forcing_now[0] - image_u) / diag_u
    new_v = inner_v + relax * (forcing_now[1] - image_v) / diag_v
    return jnp.stack([new_u, new_v])


def on_device(forcing, observed, log_friction, log_rheology, grounded):
    forcing_now = forcing[0]
    target = observed[0]
    stiffness = jnp.exp(log_rheology)
    friction_coef = grounded.astype(jnp.float32) * jnp.exp(log_friction)
    row_count = stiffness.shape[0]
    padded_stiffness = padded(stiffness, (("row", 0),), 1)
    velocity = jnp.zeros(forcing_now.shape, jnp.float32)
    saved_states = []
    for sweep_index in range(SWEEPS):
        padded_velocity = padded(velocity, (("row", 1),), 1)
        saved_states.append(padded_velocity)
        velocity = jacobi_sweep(padded_velocity, padded_stiffness, friction_coef, forcing_now)
    adjoint = velocity - target
    stiff_back = jnp.zeros(padded_stiffness.shape, jnp.float32)
    friction_back = jnp.zeros(friction_coef.shape, jnp.float32)

    def local_sweep(padded_state, padded_stiff, friction_field):
        return jacobi_sweep(padded_state, padded_stiff, friction_field, forcing_now)

    for sweep_index in reversed(range(SWEEPS)):
        unused, pullback = jax.vjp(
            local_sweep, saved_states[sweep_index], padded_stiffness, friction_coef
        )
        state_back, stiff_part, friction_part = pullback(adjoint)
        stiff_back = stiff_back + stiff_part
        friction_back = friction_back + friction_part
        if sweep_index > 0:
            edge_rows = jnp.concatenate([state_back[:, :1], state_back[:, -1:]], axis=1)
            received = padded(edge_rows, (("row", 1),), 1)
            adjoint = (
                state_back[:, 1:-1]
                + jnp.pad(received[:, :1], ((0, 0), (0, row_count - 1), (0, 0)))
                + jnp.pad(received[:, 3:], ((0, 0), (row_count - 1, 0), (0, 0)))
            )
    stiff_edges = jnp.concatenate([stiff_back[:1], stiff_back[-1:]], axis=0)
    stiff_received = padded(stiff_edges, (("row", 0),), 1)
    grad_stiff = (
        stiff_back[1:-1]
        + jnp.pad(stiff_received[:1], ((0, row_count - 1), (0, 0)))
        + jnp.pad(stiff_received[3:], ((row_count - 1, 0), (0, 0)))
    )
    gradient = jnp.stack([friction_back * friction_coef, grad_stiff * stiffness])
    parameters = jnp.stack([log_friction, log_rheology])
    cell_count = row_count * lax.axis_size("row") * gradient.shape[2]
    summed = lax.psum(gradient, "epoch")
    squares = lax.psum(jnp.sum(summed * summed, axis=(1, 2)), "row")
    grad_scale = jnp.sqrt(squares / cell_count + 1e-06)
    updated = parameters - step_size * summed / grad_scale[:, None, None]
    return (updated[0], updated[1])


def solution(mesh):
    in_specs = (
        P("epoch", None, "row", None),
        P("epoch", None, "row", None),
        P("row", None),
        P("row", None),
        P("row", None),
    )
    out_specs = (P("row", None), P("row", None))
    return jax.shard_map(
        on_device, mesh=mesh, in_specs=in_specs, out_specs=out_specs, check_vma=False
    )
```

profile of v0, /device:TPU:1, one launch (start us, length us, event | category | flops | bytes accessed | tf_op | source)
XLA Modules:
  0.0 230.6 jit_solution(5686686242233176888)
XLA Ops:
  7.2 5.1 %collective-permute-start.3 = (f32[2,1,6144]{2,1,0:T(1,128)S(1)}, f32[2,1,6144]{2,1,0:T(1,128)S(1)}, u32[]{:S(2)}, u32[]{:S(2)}) collective-permute-start(f32[2,1,6144]{2,1,0:T(1,128)S(1)} %broadcast.392), channel_id=1, source_target_pairs={{1,0},{2,1},{3,2},{4,3},{5,4},{6,5},{7,6},{8,7},{9,8},{10,9},{11,1... | collective-permute-start | bytes 147464 | tf_op jit(solution)/shard_map/ppermute | solution.py:20
  12.4 1.9 collective-permute-start.2
  14.3 1.0 exp.6
  15.3 2.2 collective-permute-start
  17.5 2.1 collective-permute-start.1
  20.4 2.3 collective-permute-done.1
  22.7 0.4 fusion.115
  23.3 0.4 fusion.117
  23.7 1.9 collective-permute-start.5
  25.7 3.6 %collective-permute-start.4 = (f32[2,1,6144]{2,1,0:T(1,128)S(1)}, f32[2,1,6144]{2,1,0:T(1,128)S(1)}, u32[]{:S(2)}, u32[]{:S(2)}) collective-permute-start(f32[2,1,6144]{2,1,0:T(1,128)S(1)} %get-tuple-element.122), channel_id=1, source_target_pairs={{0,1},{1,2},{2,3},{3,4},{4,5},{5,6},{6,7},{7,8},{8,9},{9,10},{10,1... | collective-permute-start | bytes 147464 | tf_op jit(solution)/shard_map/ppermute | solution.py:19
  29.4 1.0 collective-permute-done.4
  30.8 0.4 divide_add_fusion.3
  31.5 0.3 divide_add_fusion.2
  31.9 1.9 collective-permute-start.7
  33.8 4.2 %collective-permute-start.6 = (f32[2,1,6144]{2,1,0:T(1,128)S(1)}, f32[2,1,6144]{2,1,0:T(1,128)S(1)}, u32[]{:S(2)}, u32[]{:S(2)}) collective-permute-start(f32[2,1,6144]{2,1,0:T(1,128)S(1)} %get-tuple-element.118), channel_id=1, source_target_pairs={{0,1},{1,2},{2,3},{3,4},{4,5},{5,6},{6,7},{7,8},{8,9},{9,10},{10,1... | collective-permute-start | bytes 147464 | tf_op jit(solution)/shard_map/ppermute | solution.py:19
  38.2 1.0 collective-permute-done.6
  39.6 0.4 divide_add_fusion.1
  40.3 0.3 divide_add_fusion
  40.7 4.2 %collective-permute-start.8 = (f32[2,1,6144]{2,1,0:T(1,128)S(1)}, f32[2,1,6144]{2,1,0:T(1,128)S(1)}, u32[]{:S(2)}, u32[]{:S(2)}) collective-permute-start(f32[2,1,6144]{2,1,0:T(1,128)S(1)} %get-tuple-element.113), channel_id=1, source_target_pairs={{0,1},{1,2},{2,3},{3,4},{4,5},{5,6},{6,7},{7,8},{8,9},{9,10},{10,1... | collective-permute-start | bytes 147464 | tf_op jit(solution)/shard_map/ppermute | solution.py:19
  45.0 1.9 collective-permute-start.9
  47.0 3.4 %collective-permute-done.9 = f32[2,1,6144]{2,1,0:T(1,128)S(1)} collective-permute-done((f32[2,1,6144]{2,1,0:T(1,128)S(1)}, f32[2,1,6144]{2,1,0:T(1,128)S(1)}, u32[]{:S(2)}, u32[]{:S(2)}) %collective-permute-start.9) | collective-permute-done | bytes 49184 | tf_op jit(solution)/shard_map/ppermute | solution.py:20
  50.7 0.4 add_bitcast_fusion.1
  51.3 0.3 add_bitcast_fusion
  51.6 0.6 copy-done.5
  53.7 0.2 fusion.28
  53.9 0.2 fusion.32
  54.2 1.9 collective-permute-start.10
  56.1 2.4 %collective-permute-start.11 = (f32[2,1,6144]{2,1,0:T(1,128)S(1)}, f32[2,1,6144]{2,1,0:T(1,128)S(1)}, u32[]{:S(2)}, u32[]{:S(2)}) collective-permute-start(f32[2,1,6144]{2,1,0:T(1,128)S(1)} %get-tuple-element.93), channel_id=1, source_target_pairs={{1,0},{2,1},{3,2},{4,3},{5,4},{6,5},{7,6},{8,7},{9,8},{10,9},{11,1... | collective-permute-start | bytes 147464 | tf_op jit(solution)/shard_map/ppermute | solution.py:20
  58.6 3.3 %collective-permute-done.11 = f32[2,1,6144]{2,1,0:T(1,128)S(1)} collective-permute-done((f32[2,1,6144]{2,1,0:T(1,128)S(1)}, f32[2,1,6144]{2,1,0:T(1,128)S(1)}, u32[]{:S(2)}, u32[]{:S(2)}) %collective-permute-start.11) | collective-permute-done | bytes 49184 | tf_op jit(solution)/shard_map/ppermute | solution.py:20
  63.8 1.9 collective-permute-start.12
  65.8 2.4 %collective-permute-start.13 = (f32[2,1,6144]{2,1,0:T(1,128)S(1)}, f32[2,1,6144]{2,1,0:T(1,128)S(1)}, u32[]{:S(2)}, u32[]{:S(2)}) collective-permute-start(f32[2,1,6144]{2,1,0:T(1,128)S(1)} %get-tuple-element.91), channel_id=1, source_target_pairs={{1,0},{2,1},{3,2},{4,3},{5,4},{6,5},{7,6},{8,7},{9,8},{10,9},{11,1... | collective-permute-start | bytes 147464 | tf_op jit(solution)/shard_map/ppermute | solution.py:20
  68.2 6.1 %collective-permute-done.13 = f32[2,1,6144]{2,1,0:T(1,128)S(1)} collective-permute-done((f32[2,1,6144]{2,1,0:T(1,128)S(1)}, f32[2,1,6144]{2,1,0:T(1,128)S(1)}, u32[]{:S(2)}, u32[]{:S(2)}) %collective-permute-start.13) | collective-permute-done | bytes 49184 | tf_op jit(solution)/shard_map/ppermute | solution.py:20
  75.7 0.2 fusion.12
  76.0 0.2 fusion.16
  76.3 2.3 %collective-permute-start.14 = (f32[2,1,6144]{2,1,0:T(1,128)S(1)}, f32[2,1,6144]{2,1,0:T(1,128)S(1)}, u32[]{:S(2)}, u32[]{:S(2)}) collective-permute-start(f32[2,1,6144]{2,1,0:T(1,128)S(1)} %get-tuple-element.88), channel_id=1, source_target_pairs={{0,1},{1,2},{2,3},{3,4},{4,5},{5,6},{6,7},{7,8},{8,9},{9,10},{10,1... | collective-permute-start | bytes 147464 | tf_op jit(solution)/shard_map/ppermute | solution.py:19
  78.6 2.2 collective-permute-start.15
  80.8 7.6 %collective-permute-done.15 = f32[2,1,6144]{2,1,0:T(1,128)S(1)} collective-permute-done((f32[2,1,6144]{2,1,0:T(1,128)S(1)}, f32[2,1,6144]{2,1,0:T(1,128)S(1)}, u32[]{:S(2)}, u32[]{:S(2)}) %collective-permute-start.15) | collective-permute-done | bytes 49184 | tf_op jit(solution)/shard_map/ppermute | solution.py:20
  88.5 0.5 multiply_bitcast_fusion
  90.8 0.2 fusion.62
  91.2 1.9 collective-permute-start.16
  93.1 2.4 %collective-permute-start.17 = (f32[1,6144]{1,0:T(1,128)S(1)}, f32[1,6144]{1,0:T(1,128)S(1)}, u32[]{:S(2)}, u32[]{:S(2)}) collective-permute-start(f32[1,6144]{1,0:T(1,128)S(1)} %add_add_fusion.3), channel_id=1, source_target_pairs={{1,0},{2,1},{3,2},{4,3},{5,4},{6,5},{7,6},{8,7},{9,8},{10,9},{11,1... | collective-permute-start | bytes 73736 | tf_op jit(solution)/shard_map/ppermute | solution.py:20
  95.5 0.3 add_add_fusion
  95.9 3.6 %collective-permute-done.17 = f32[1,6144]{1,0:T(1,128)S(1)} collective-permute-done((f32[1,6144]{1,0:T(1,128)S(1)}, f32[1,6144]{1,0:T(1,128)S(1)}, u32[]{:S(2)}, u32[]{:S(2)}) %collective-permute-start.17) | collective-permute-done | bytes 24608 | tf_op jit(solution)/shard_map/ppermute | solution.py:20
  99.5 0.8 pad_maximum_fusion
  100.4 95.9 %all-reduce.164.cloned.1.call-done = f32[2,8,6144]{2,1,0:T(8,128)} async-done(((f32[2,8,6144]{2,1,0:T(8,128)}), f32[2,8,6144]{2,1,0:T(8,128)}) %all-reduce.164.cloned.1.call-update) | async-done | bytes 393232 | tf_op jit(solution)/shard_map/psum | solution.py:118
  196.3 1.2 multiply_reduce_fusion
  197.5 25.3 %psum.15 = f32[2]{0:T(128)S(1)} all-reduce(f32[2]{0:T(128)S(1)} %multiply_reduce_fusion), channel_id=1, replica_groups=mesh['epoch'=16,'row'=16] {'row'}, use_global_device_ids=true, to_apply=%region_2.3 | all-reduce | flops 2 | bytes 16 | tf_op jit(solution)/shard_map/psum | solution.py:119
  223.0 0.8 slice_bitcast_fusion
  (114 shorter events, 10.1 us)
Async XLA Ops:
  7.2 189.2 %all-reduce.164.cloned.1.call-start = ((), (), s32[]{:S(2)}) async-start(), calls=%async_computation | async-start | bytes 786432 | tf_op jit(solution)/shard_map/psum | solution.py:118
  7.2 12.9 %collective-permute-start.3 = (f32[2,1,6144]{2,1,0:T(1,128)S(1)}, f32[2,1,6144]{2,1,0:T(1,128)S(1)}, u32[]{:S(2)}, u32[]{:S(2)}) collective-permute-start(f32[2,1,6144]{2,1,0:T(1,128)S(1)} %broadcast.392), channel_id=1, source_target_pairs={{1,0},{2,1},{3,2},{4,3},{5,4},{6,5},{7,6},{8,7},{9,8},{10,9},{11,1... | collective-permute-start | bytes 147464 | tf_op jit(solution)/shard_map/ppermute | solution.py:20
  12.4 7.5 %collective-permute-start.2 = (f32[2,1,6144]{2,1,0:T(1,128)S(1)}, f32[2,1,6144]{2,1,0:T(1,128)S(1)}, u32[]{:S(2)}, u32[]{:S(2)}) collective-permute-start(f32[2,1,6144]{2,1,0:T(1,128)S(1)} %broadcast.392), channel_id=1, source_target_pairs={{0,1},{1,2},{2,3},{3,4},{4,5},{5,6},{6,7},{7,8},{8,9},{9,10},{10,1... | collective-permute-start | bytes 147464 | tf_op jit(solution)/shard_map/ppermute | solution.py:19
  15.3 5.1 %collective-permute-start = (f32[1,6144]{1,0:T(1,128)S(1)}, f32[1,6144]{1,0:T(1,128)S(1)}, u32[]{:S(2)}, u32[]{:S(2)}) collective-permute-start(f32[1,6144]{1,0:T(1,128)S(1)} %get-tuple-element.211), channel_id=1, source_target_pairs={{0,1},{1,2},{2,3},{3,4},{4,5},{5,6},{6,7},{7,8},{8,9},{9,10},{10,1... | collective-permute-start | bytes 73736 | tf_op jit(solution)/shard_map/ppermute | solution.py:19
  17.5 5.1 %collective-permute-start.1 = (f32[1,6144]{1,0:T(1,128)S(1)}, f32[1,6144]{1,0:T(1,128)S(1)}, u32[]{:S(2)}, u32[]{:S(2)}) collective-permute-start(f32[1,6144]{1,0:T(1,128)S(1)} %get-tuple-element.212), channel_id=1, source_target_pairs={{1,0},{2,1},{3,2},{4,3},{5,4},{6,5},{7,6},{8,7},{9,8},{10,9},{11,1... | collective-permute-start | bytes 73736 | tf_op jit(solution)/shard_map/ppermute | solution.py:20
  20.2 2.5 %copy-start = (f32[8,6144]{1,0:T(8,128)S(1)}, f32[8,6144]{1,0:T(8,128)}, u32[]{:S(2)}) copy-start(f32[8,6144]{1,0:T(8,128)} %param.8) | copy-start | bytes 589828
  20.2 2.5 %copy-start.1 = (f32[1,2,8,6144]{3,2,1,0:T(8,128)S(1)}, f32[1,2,8,6144]{3,2,1,0:T(8,128)}, u32[]{:S(2)}) copy-start(f32[1,2,8,6144]{3,2,1,0:T(8,128)} %param.5) | copy-start | bytes 1179652
  20.2 2.5 %copy-start.2 = (f32[8,6144]{1,0:T(8,128)S(1)}, f32[8,6144]{1,0:T(8,128)}, u32[]{:S(2)}) copy-start(f32[8,6144]{1,0:T(8,128)} %param.7) | copy-start | bytes 589828
  20.2 2.5 %copy-start.3 = (s32[8,6144]{1,0:T(8,128)S(1)}, s32[8,6144]{1,0:T(8,128)}, u32[]{:S(2)}) copy-start(s32[8,6144]{1,0:T(8,128)} %param.9) | copy-start | bytes 589828
  23.7 5.7 %collective-permute-start.5 = (f32[2,1,6144]{2,1,0:T(1,128)S(1)}, f32[2,1,6144]{2,1,0:T(1,128)S(1)}, u32[]{:S(2)}, u32[]{:S(2)}) collective-permute-start(f32[2,1,6144]{2,1,0:T(1,128)S(1)} %get-tuple-element.121), channel_id=1, source_target_pairs={{1,0},{2,1},{3,2},{4,3},{5,4},{6,5},{7,6},{8,7},{9,8},{10,9},{11,1... | collective-permute-start | bytes 147464 | tf_op jit(solution)/shard_map/ppermute | solution.py:20
  25.7 4.8 %collective-permute-start.4 = (f32[2,1,6144]{2,1,0:T(1,128)S(1)}, f32[2,1,6144]{2,1,0:T(1,128)S(1)}, u32[]{:S(2)}, u32[]{:S(2)}) collective-permute-start(f32[2,1,6144]{2,1,0:T(1,128)S(1)} %get-tuple-element.122), channel_id=1, source_target_pairs={{0,1},{1,2},{2,3},{3,4},{4,5},{5,6},{6,7},{7,8},{8,9},{9,10},{10,1... | collective-permute-start | bytes 147464 | tf_op jit(solution)/shard_map/ppermute | solution.py:19
  31.9 6.3 %collective-permute-start.7 = (f32[2,1,6144]{2,1,0:T(1,128)S(1)}, f32[2,1,6144]{2,1,0:T(1,128)S(1)}, u32[]{:S(2)}, u32[]{:S(2)}) collective-permute-start(f32[2,1,6144]{2,1,0:T(1,128)S(1)} %get-tuple-element.117), channel_id=1, source_target_pairs={{1,0},{2,1},{3,2},{4,3},{5,4},{6,5},{7,6},{8,7},{9,8},{10,9},{11,1... | collective-permute-start | bytes 147464 | tf_op jit(solution)/shard_map/ppermute | solution.py:20
  33.8 5.4 %collective-permute-start.6 = (f32[2,1,6144]{2,1,0:T(1,128)S(1)}, f32[2,1,6144]{2,1,0:T(1,128)S(1)}, u32[]{:S(2)}, u32[]{:S(2)}) collective-permute-start(f32[2,1,6144]{2,1,0:T(1,128)S(1)} %get-tuple-element.118), channel_id=1, source_target_pairs={{0,1},{1,2},{2,3},{3,4},{4,5},{5,6},{6,7},{7,8},{8,9},{9,10},{10,1... | collective-permute-start | bytes 147464 | tf_op jit(solution)/shard_map/ppermute | solution.py:19
  40.7 6.3 %collective-permute-start.8 = (f32[2,1,6144]{2,1,0:T(1,128)S(1)}, f32[2,1,6144]{2,1,0:T(1,128)S(1)}, u32[]{:S(2)}, u32[]{:S(2)}) collective-permute-start(f32[2,1,6144]{2,1,0:T(1,128)S(1)} %get-tuple-element.113), channel_id=1, source_target_pairs={{0,1},{1,2},{2,3},{3,4},{4,5},{5,6},{6,7},{7,8},{8,9},{9,10},{10,1... | collective-permute-start | bytes 147464 | tf_op jit(solution)/shard_map/ppermute | solution.py:19
  45.0 5.4 %collective-permute-start.9 = (f32[2,1,6144]{2,1,0:T(1,128)S(1)}, f32[2,1,6144]{2,1,0:T(1,128)S(1)}, u32[]{:S(2)}, u32[]{:S(2)}) collective-permute-start(f32[2,1,6144]{2,1,0:T(1,128)S(1)} %get-tuple-element.114), channel_id=1, source_target_pairs={{1,0},{2,1},{3,2},{4,3},{5,4},{6,5},{7,6},{8,7},{9,8},{10,9},{11,1... | collective-permute-start | bytes 147464 | tf_op jit(solution)/shard_map/ppermute | solution.py:20
  51.3 1.0 copy-start.5
  54.2 4.3 %collective-permute-start.10 = (f32[2,1,6144]{2,1,0:T(1,128)S(1)}, f32[2,1,6144]{2,1,0:T(1,128)S(1)}, u32[]{:S(2)}, u32[]{:S(2)}) collective-permute-start(f32[2,1,6144]{2,1,0:T(1,128)S(1)} %get-tuple-element.92), channel_id=1, source_target_pairs={{0,1},{1,2},{2,3},{3,4},{4,5},{5,6},{6,7},{7,8},{8,9},{9,10},{10,1... | collective-permute-start | bytes 147464 | tf_op jit(solution)/shard_map/ppermute | solution.py:19
  56.1 5.7 %collective-permute-start.11 = (f32[2,1,6144]{2,1,0:T(1,128)S(1)}, f32[2,1,6144]{2,1,0:T(1,128)S(1)}, u32[]{:S(2)}, u32[]{:S(2)}) collective-permute-start(f32[2,1,6144]{2,1,0:T(1,128)S(1)} %get-tuple-element.93), channel_id=1, source_target_pairs={{1,0},{2,1},{3,2},{4,3},{5,4},{6,5},{7,6},{8,7},{9,8},{10,9},{11,1... | collective-permute-start | bytes 147464 | tf_op jit(solution)/shard_map/ppermute | solution.py:20
  63.8 4.3 %collective-permute-start.12 = (f32[2,1,6144]{2,1,0:T(1,128)S(1)}, f32[2,1,6144]{2,1,0:T(1,128)S(1)}, u32[]{:S(2)}, u32[]{:S(2)}) collective-permute-start(f32[2,1,6144]{2,1,0:T(1,128)S(1)} %get-tuple-element.90), channel_id=1, source_target_pairs={{0,1},{1,2},{2,3},{3,4},{4,5},{5,6},{6,7},{7,8},{8,9},{9,10},{10,1... | collective-permute-start | bytes 147464 | tf_op jit(solution)/shard_map/ppermute | solution.py:19
  65.8 8.5 %collective-permute-start.13 = (f32[2,1,6144]{2,1,0:T(1,128)S(1)}, f32[2,1,6144]{2,1,0:T(1,128)S(1)}, u32[]{:S(2)}, u32[]{:S(2)}) collective-permute-start(f32[2,1,6144]{2,1,0:T(1,128)S(1)} %get-tuple-element.91), channel_id=1, source_target_pairs={{1,0},{2,1},{3,2},{4,3},{5,4},{6,5},{7,6},{8,7},{9,8},{10,9},{11,1... | collective-permute-start | bytes 147464 | tf_op jit(solution)/shard_map/ppermute | solution.py:20
  76.3 4.5 %collective-permute-start.14 = (f32[2,1,6144]{2,1,0:T(1,128)S(1)}, f32[2,1,6144]{2,1,0:T(1,128)S(1)}, u32[]{:S(2)}, u32[]{:S(2)}) collective-permute-start(f32[2,1,6144]{2,1,0:T(1,128)S(1)} %get-tuple-element.88), channel_id=1, source_target_pairs={{0,1},{1,2},{2,3},{3,4},{4,5},{5,6},{6,7},{7,8},{8,9},{9,10},{10,1... | collective-permute-start | bytes 147464 | tf_op jit(solution)/shard_map/ppermute | solution.py:19
  78.6 9.8 %collective-permute-start.15 = (f32[2,1,6144]{2,1,0:T(1,128)S(1)}, f32[2,1,6144]{2,1,0:T(1,128)S(1)}, u32[]{:S(2)}, u32[]{:S(2)}) collective-permute-start(f32[2,1,6144]{2,1,0:T(1,128)S(1)} %get-tuple-element.89), channel_id=1, source_target_pairs={{1,0},{2,1},{3,2},{4,3},{5,4},{6,5},{7,6},{8,7},{9,8},{10,9},{11,1... | collective-permute-start | bytes 147464 | tf_op jit(solution)/shard_map/ppermute | solution.py:20
  91.2 4.7 %collective-permute-start.16 = (f32[1,6144]{1,0:T(1,128)S(1)}, f32[1,6144]{1,0:T(1,128)S(1)}, u32[]{:S(2)}, u32[]{:S(2)}) collective-permute-start(f32[1,6144]{1,0:T(1,128)S(1)} %add_add_fusion.4), channel_id=1, source_target_pairs={{0,1},{1,2},{2,3},{3,4},{4,5},{5,6},{6,7},{7,8},{8,9},{9,10},{10,1... | collective-permute-start | bytes 73736 | tf_op jit(solution)/shard_map/ppermute | solution.py:19
  93.1 6.4 %collective-permute-start.17 = (f32[1,6144]{1,0:T(1,128)S(1)}, f32[1,6144]{1,0:T(1,128)S(1)}, u32[]{:S(2)}, u32[]{:S(2)}) collective-permute-start(f32[1,6144]{1,0:T(1,128)S(1)} %add_add_fusion.3), channel_id=1, source_target_pairs={{1,0},{2,1},{3,2},{4,3},{5,4},{6,5},{7,6},{8,7},{9,8},{10,9},{11,1... | collective-permute-start | bytes 73736 | tf_op jit(solution)/shard_map/ppermute | solution.py:20
  196.3 26.5 %copy-start.4 = (f32[2,8,6144]{2,1,0:T(8,128)S(1)}, f32[2,8,6144]{2,1,0:T(8,128)}, u32[]{:S(2)}) copy-start(f32[2,8,6144]{2,1,0:T(8,128)} %all-reduce.164.cloned.1.call-done) | copy-start | bytes 1179652
Sparse Core Ops, SparseCore 0:
  100.5 95.7 all-reduce.163
where the time goes:
time: 231 us
  waiting for transfers between devices  124 us (54%)
  starting transfers between devices  46.8 us (20%)
  blocking collectives  25.3 us (11%)
  between operations  14.9 us (6%)
  other arithmetic  12.6 us (5%)
  local copies, waits for them, and re-layouts  6.81 us (3%)
    psum x1, waiting for transfers between devices, on_device(): summed = lax.psum(gradient, 'epoch')  95.9 us
    ppermute x9, waiting for transfers between devices, padded(): after = lax.ppermute(first, axis, down)  26.1 us
    psum x1, blocking collectives, on_device(): squares = lax.psum(jnp.sum(summed * summed, axis=(1, 2)), 'row')  25.3 us
    ppermute x9, starting transfers between devices, padded(): before = lax.ppermute(last, axis, up)  24.3 us
    ppermute x9, starting transfers between devices, padded(): after = lax.ppermute(first, axis, down)  22.4 us
  transfers between devices with their start and end apart: 19, of which 9 were waited for; matrix products, arithmetic and copies ran while one was open for 1% of the time, Pallas kernels for 0%

commit v1 on v0

--- a/solution.py
+++ b/solution.py
@@ -115,7 +115,7 @@
     gradient = jnp.stack([friction_back * friction_coef, grad_stiff * stiffness])
     parameters = jnp.stack([log_friction, log_rheology])
     cell_count = row_count * lax.axis_size("row") * gradient.shape[2]
-    summed = lax.psum(gradient, "epoch")
+    summed = jnp.sum(lax.all_gather(gradient, "epoch"), axis=0)
     squares = lax.psum(jnp.sum(summed * summed, axis=(1, 2)), "row")
     grad_scale = jnp.sqrt(squares / cell_count + 1e-06)
     updated = parameters - step_size * summed / grad_scale[:, None, None]

time: 231 us -> 207 us (0.90)
  waiting for transfers between devices: 124 us -> 97.5 us
  other arithmetic: 12.6 us -> 15.5 us
    psum x1 -> x0, waiting for transfers between devices: 95.9 us -> none  [on_device(): summed = lax.psum(gradient, 'epoch')]
    all_gather x0 -> x1, waiting for transfers between devices: none -> 69.2 us  [on_device(): summed = jnp.sum(lax.all_gather(gradient, 'epoch'), axis=0)]
    reduce_sum x0 -> x1, other arithmetic: none -> 3.11 us  [on_device(): summed = jnp.sum(lax.all_gather(gradient, 'epoch'), axis=0)]
where the time goes in v1:
time: 207 us; the launch traced here: 205 us
  waiting for transfers between devices  97.5 us (47%)
  starting transfers between devices  47.1 us (23%)
  blocking collectives  24 us (12%)
  other arithmetic  15.5 us (7%)
  between operations  15 us (7%)
  local copies, waits for them, and re-layouts  6.16 us (3%)
    all_gather x1, waiting for transfers between devices, on_device(): summed = jnp.sum(lax.all_gather(gradient, 'epoch'), axis=0)  69.2 us
    ppermute x9, waiting for transfers between devices, padded(): after = lax.ppermute(first, axis, down)  26.2 us
    ppermute x9, starting transfers between devices, padded(): before = lax.ppermute(last, axis, up)  24.5 us
    psum x1, blocking collectives, on_device(): squares = lax.psum(jnp.sum(summed * summed, axis=(1, 2)), 'row')  24 us
    ppermute x9, starting transfers between devices, padded(): after = lax.ppermute(first, axis, down)  22.6 us
  transfers between devices with their start and end apart: 19, of which 9 were waited for; matrix products, arithmetic and copies ran while one was open for 1% of the time, Pallas kernels for 0%

profile of v1, /device:TPU:1, one launch (start us, length us, event | category | flops | bytes accessed | tf_op | source)
XLA Modules:
  0.0 205.2 jit_solution(14763147367769868228)
XLA Ops:
  7.3 5.3 %collective-permute-start.3 = (f32[2,1,6144]{2,1,0:T(1,128)S(1)}, f32[2,1,6144]{2,1,0:T(1,128)S(1)}, u32[]{:S(2)}, u32[]{:S(2)}) collective-permute-start(f32[2,1,6144]{2,1,0:T(1,128)S(1)} %broadcast.392), channel_id=1, source_target_pairs={{1,0},{2,1},{3,2},{4,3},{5,4},{6,5},{7,6},{8,7},{9,8},{10,9},{11,1... | collective-permute-start | bytes 147464 | tf_op jit(solution)/shard_map/ppermute | solution.py:20
  12.6 1.9 collective-permute-start.2
  14.5 1.0 exp.6
  15.5 2.2 %collective-permute-start = (f32[1,6144]{1,0:T(1,128)S(1)}, f32[1,6144]{1,0:T(1,128)S(1)}, u32[]{:S(2)}, u32[]{:S(2)}) collective-permute-start(f32[1,6144]{1,0:T(1,128)S(1)} %get-tuple-element.211), channel_id=1, source_target_pairs={{0,1},{1,2},{2,3},{3,4},{4,5},{5,6},{6,7},{7,8},{8,9},{9,10},{10,1... | collective-permute-start | bytes 73736 | tf_op jit(solution)/shard_map/ppermute | solution.py:19
  17.7 2.1 %collective-permute-start.1 = (f32[1,6144]{1,0:T(1,128)S(1)}, f32[1,6144]{1,0:T(1,128)S(1)}, u32[]{:S(2)}, u32[]{:S(2)}) collective-permute-start(f32[1,6144]{1,0:T(1,128)S(1)} %get-tuple-element.212), channel_id=1, source_target_pairs={{1,0},{2,1},{3,2},{4,3},{5,4},{6,5},{7,6},{8,7},{9,8},{10,9},{11,1... | collective-permute-start | bytes 73736 | tf_op jit(solution)/shard_map/ppermute | solution.py:20
  20.5 2.3 %collective-permute-done.1 = f32[1,6144]{1,0:T(1,128)S(1)} collective-permute-done((f32[1,6144]{1,0:T(1,128)S(1)}, f32[1,6144]{1,0:T(1,128)S(1)}, u32[]{:S(2)}, u32[]{:S(2)}) %collective-permute-start.1) | collective-permute-done | bytes 24608 | tf_op jit(solution)/shard_map/ppermute | solution.py:20
  22.8 1.6 fusion.115
  24.6 0.4 fusion.117
  25.1 1.9 collective-permute-start.5
  27.0 3.6 %collective-permute-start.4 = (f32[2,1,6144]{2,1,0:T(1,128)S(1)}, f32[2,1,6144]{2,1,0:T(1,128)S(1)}, u32[]{:S(2)}, u32[]{:S(2)}) collective-permute-start(f32[2,1,6144]{2,1,0:T(1,128)S(1)} %get-tuple-element.122), channel_id=1, source_target_pairs={{0,1},{1,2},{2,3},{3,4},{4,5},{5,6},{6,7},{7,8},{8,9},{9,10},{10,1... | collective-permute-start | bytes 147464 | tf_op jit(solution)/shard_map/ppermute | solution.py:19
  30.8 1.0 collective-permute-done.4
  32.1 0.3 divide_add_fusion.3
  32.9 0.3 divide_add_fusion.2
  33.2 1.9 collective-permute-start.7
  35.2 4.2 %collective-permute-start.6 = (f32[2,1,6144]{2,1,0:T(1,128)S(1)}, f32[2,1,6144]{2,1,0:T(1,128)S(1)}, u32[]{:S(2)}, u32[]{:S(2)}) collective-permute-start(f32[2,1,6144]{2,1,0:T(1,128)S(1)} %get-tuple-element.118), channel_id=1, source_target_pairs={{0,1},{1,2},{2,3},{3,4},{4,5},{5,6},{6,7},{7,8},{8,9},{9,10},{10,1... | collective-permute-start | bytes 147464 | tf_op jit(solution)/shard_map/ppermute | solution.py:19
  39.5 1.0 collective-permute-done.6
  40.9 0.3 divide_add_fusion.1
  41.6 0.3 divide_add_fusion
  42.0 4.4 %collective-permute-start.8 = (f32[2,1,6144]{2,1,0:T(1,128)S(1)}, f32[2,1,6144]{2,1,0:T(1,128)S(1)}, u32[]{:S(2)}, u32[]{:S(2)}) collective-permute-start(f32[2,1,6144]{2,1,0:T(1,128)S(1)} %get-tuple-element.113), channel_id=1, source_target_pairs={{0,1},{1,2},{2,3},{3,4},{4,5},{5,6},{6,7},{7,8},{8,9},{9,10},{10,1... | collective-permute-start | bytes 147464 | tf_op jit(solution)/shard_map/ppermute | solution.py:19
  46.4 1.9 collective-permute-start.9
  48.4 3.4 %collective-permute-done.9 = f32[2,1,6144]{2,1,0:T(1,128)S(1)} collective-permute-done((f32[2,1,6144]{2,1,0:T(1,128)S(1)}, f32[2,1,6144]{2,1,0:T(1,128)S(1)}, u32[]{:S(2)}, u32[]{:S(2)}) %collective-permute-start.9) | collective-permute-done | bytes 49184 | tf_op jit(solution)/shard_map/ppermute | solution.py:20
  52.1 0.3 add_bitcast_fusion.1
  52.7 0.3 add_bitcast_fusion
  54.4 0.2 fusion.28
  54.6 0.2 fusion.32
  54.9 1.9 collective-permute-start.10
  56.9 2.4 %collective-permute-start.11 = (f32[2,1,6144]{2,1,0:T(1,128)S(1)}, f32[2,1,6144]{2,1,0:T(1,128)S(1)}, u32[]{:S(2)}, u32[]{:S(2)}) collective-permute-start(f32[2,1,6144]{2,1,0:T(1,128)S(1)} %get-tuple-element.93), channel_id=1, source_target_pairs={{1,0},{2,1},{3,2},{4,3},{5,4},{6,5},{7,6},{8,7},{9,8},{10,9},{11,1... | collective-permute-start | bytes 147464 | tf_op jit(solution)/shard_map/ppermute | solution.py:20
  59.3 3.3 %collective-permute-done.11 = f32[2,1,6144]{2,1,0:T(1,128)S(1)} collective-permute-done((f32[2,1,6144]{2,1,0:T(1,128)S(1)}, f32[2,1,6144]{2,1,0:T(1,128)S(1)}, u32[]{:S(2)}, u32[]{:S(2)}) %collective-permute-start.11) | collective-permute-done | bytes 49184 | tf_op jit(solution)/shard_map/ppermute | solution.py:20
  64.0 0.2 fusion.20
  64.2 0.2 fusion.24
  64.5 1.9 collective-permute-start.12
  66.5 2.4 %collective-permute-start.13 = (f32[2,1,6144]{2,1,0:T(1,128)S(1)}, f32[2,1,6144]{2,1,0:T(1,128)S(1)}, u32[]{:S(2)}, u32[]{:S(2)}) collective-permute-start(f32[2,1,6144]{2,1,0:T(1,128)S(1)} %get-tuple-element.91), channel_id=1, source_target_pairs={{1,0},{2,1},{3,2},{4,3},{5,4},{6,5},{7,6},{8,7},{9,8},{10,9},{11,1... | collective-permute-start | bytes 147464 | tf_op jit(solution)/shard_map/ppermute | solution.py:20
  68.9 6.1 %collective-permute-done.13 = f32[2,1,6144]{2,1,0:T(1,128)S(1)} collective-permute-done((f32[2,1,6144]{2,1,0:T(1,128)S(1)}, f32[2,1,6144]{2,1,0:T(1,128)S(1)}, u32[]{:S(2)}, u32[]{:S(2)}) %collective-permute-start.13) | collective-permute-done | bytes 49184 | tf_op jit(solution)/shard_map/ppermute | solution.py:20
  76.4 0.2 fusion.12
  76.6 0.2 fusion.16
  76.9 2.3 %collective-permute-start.14 = (f32[2,1,6144]{2,1,0:T(1,128)S(1)}, f32[2,1,6144]{2,1,0:T(1,128)S(1)}, u32[]{:S(2)}, u32[]{:S(2)}) collective-permute-start(f32[2,1,6144]{2,1,0:T(1,128)S(1)} %get-tuple-element.88), channel_id=1, source_target_pairs={{0,1},{1,2},{2,3},{3,4},{4,5},{5,6},{6,7},{7,8},{8,9},{9,10},{10,1... | collective-permute-start | bytes 147464 | tf_op jit(solution)/shard_map/ppermute | solution.py:19
  79.3 2.2 %collective-permute-start.15 = (f32[2,1,6144]{2,1,0:T(1,128)S(1)}, f32[2,1,6144]{2,1,0:T(1,128)S(1)}, u32[]{:S(2)}, u32[]{:S(2)}) collective-permute-start(f32[2,1,6144]{2,1,0:T(1,128)S(1)} %get-tuple-element.89), channel_id=1, source_target_pairs={{1,0},{2,1},{3,2},{4,3},{5,4},{6,5},{7,6},{8,7},{9,8},{10,9},{11,1... | collective-permute-start | bytes 147464 | tf_op jit(solution)/shard_map/ppermute | solution.py:20
  81.5 7.6 %collective-permute-done.15 = f32[2,1,6144]{2,1,0:T(1,128)S(1)} collective-permute-done((f32[2,1,6144]{2,1,0:T(1,128)S(1)}, f32[2,1,6144]{2,1,0:T(1,128)S(1)}, u32[]{:S(2)}, u32[]{:S(2)}) %collective-permute-start.15) | collective-permute-done | bytes 49184 | tf_op jit(solution)/shard_map/ppermute | solution.py:20
  89.1 0.5 multiply_bitcast_fusion
  91.8 1.9 collective-permute-start.16
  93.7 2.4 %collective-permute-start.17 = (f32[1,6144]{1,0:T(1,128)S(1)}, f32[1,6144]{1,0:T(1,128)S(1)}, u32[]{:S(2)}, u32[]{:S(2)}) collective-permute-start(f32[1,6144]{1,0:T(1,128)S(1)} %add_add_fusion.3), channel_id=1, source_target_pairs={{1,0},{2,1},{3,2},{4,3},{5,4},{6,5},{7,6},{8,7},{9,8},{10,9},{11,1... | collective-permute-start | bytes 73736 | tf_op jit(solution)/shard_map/ppermute | solution.py:20
  96.1 0.3 add_add_fusion
  96.5 3.6 %collective-permute-done.17 = f32[1,6144]{1,0:T(1,128)S(1)} collective-permute-done((f32[1,6144]{1,0:T(1,128)S(1)}, f32[1,6144]{1,0:T(1,128)S(1)}, u32[]{:S(2)}, u32[]{:S(2)}) %collective-permute-start.17) | collective-permute-done | bytes 24608 | tf_op jit(solution)/shard_map/ppermute | solution.py:20
  100.2 0.8 pad_maximum_fusion
  101.0 69.2 %all-gather.3.cloned.1.call-done = f32[32,8,6144]{2,1,0:T(8,128)} async-done(((f32[2,8,6144]{2,1,0:T(8,128)}), f32[32,8,6144]{2,1,0:T(8,128)}) %all-gather.3.cloned.1.call-update) | async-done | bytes 6291472 | tf_op jit(solution)/shard_map/all_gather | solution.py:118
  170.1 3.1 %reduce_sum.18 = f32[2,8,6144]{2,1,0:T(8,128)S(1)} reduce(f32[16,2,8,6144]{3,2,1,0:T(8,128)} %bitcast.230, f32[]{:T(128)} %constant.68.clone.1), dimensions={0}, to_apply=%region_0.1 | reduce | flops 1474560 | bytes 6684676 | tf_op jit(solution)/shard_map/reduce_sum | solution.py:118
  173.4 24.0 %psum.7 = f32[2]{0:T(128)S(1)} all-reduce(f32[2]{0:T(128)S(1)} %multiply_reduce_fusion), channel_id=1, replica_groups=mesh['epoch'=16,'row'=16] {'row'}, use_global_device_ids=true, to_apply=%region_2.3 | all-reduce | flops 2 | bytes 16 | tf_op jit(solution)/shard_map/psum | solution.py:119
  197.6 0.8 slice_bitcast_fusion
  (113 shorter events, 9.9 us)
Async XLA Ops:
  7.2 17.4 %copy-start.1 = (f32[1,2,8,6144]{3,2,1,0:T(8,128)S(1)}, f32[1,2,8,6144]{3,2,1,0:T(8,128)}, u32[]{:S(2)}) copy-start(f32[1,2,8,6144]{3,2,1,0:T(8,128)} %param.5) | copy-start | bytes 1179652
  7.2 17.4 %copy-start.2 = (f32[8,6144]{1,0:T(8,128)S(1)}, f32[8,6144]{1,0:T(8,128)}, u32[]{:S(2)}) copy-start(f32[8,6144]{1,0:T(8,128)} %param.7) | copy-start | bytes 589828
  7.2 17.4 %copy-start.3 = (s32[8,6144]{1,0:T(8,128)S(1)}, s32[8,6144]{1,0:T(8,128)}, u32[]{:S(2)}) copy-start(s32[8,6144]{1,0:T(8,128)} %param.9) | copy-start | bytes 589828
  7.2 162.9 %all-gather.3.cloned.1.call-start = ((), (), s32[]{:S(2)}) async-start(), calls=%async_computation | async-start | bytes 6684672 | tf_op jit(solution)/shard_map/all_gather | solution.py:118
  7.3 13.0 %collective-permute-start.3 = (f32[2,1,6144]{2,1,0:T(1,128)S(1)}, f32[2,1,6144]{2,1,0:T(1,128)S(1)}, u32[]{:S(2)}, u32[]{:S(2)}) collective-permute-start(f32[2,1,6144]{2,1,0:T(1,128)S(1)} %broadcast.392), channel_id=1, source_target_pairs={{1,0},{2,1},{3,2},{4,3},{5,4},{6,5},{7,6},{8,7},{9,8},{10,9},{11,1... | collective-permute-start | bytes 147464 | tf_op jit(solution)/shard_map/ppermute | solution.py:20
  12.6 7.5 %collective-permute-start.2 = (f32[2,1,6144]{2,1,0:T(1,128)S(1)}, f32[2,1,6144]{2,1,0:T(1,128)S(1)}, u32[]{:S(2)}, u32[]{:S(2)}) collective-permute-start(f32[2,1,6144]{2,1,0:T(1,128)S(1)} %broadcast.392), channel_id=1, source_target_pairs={{0,1},{1,2},{2,3},{3,4},{4,5},{5,6},{6,7},{7,8},{8,9},{9,10},{10,1... | collective-permute-start | bytes 147464 | tf_op jit(solution)/shard_map/ppermute | solution.py:19
  15.5 5.0 %collective-permute-start = (f32[1,6144]{1,0:T(1,128)S(1)}, f32[1,6144]{1,0:T(1,128)S(1)}, u32[]{:S(2)}, u32[]{:S(2)}) collective-permute-start(f32[1,6144]{1,0:T(1,128)S(1)} %get-tuple-element.211), channel_id=1, source_target_pairs={{0,1},{1,2},{2,3},{3,4},{4,5},{5,6},{6,7},{7,8},{8,9},{9,10},{10,1... | collective-permute-start | bytes 73736 | tf_op jit(solution)/shard_map/ppermute | solution.py:19
  17.7 5.1 %collective-permute-start.1 = (f32[1,6144]{1,0:T(1,128)S(1)}, f32[1,6144]{1,0:T(1,128)S(1)}, u32[]{:S(2)}, u32[]{:S(2)}) collective-permute-start(f32[1,6144]{1,0:T(1,128)S(1)} %get-tuple-element.212), channel_id=1, source_target_pairs={{1,0},{2,1},{3,2},{4,3},{5,4},{6,5},{7,6},{8,7},{9,8},{10,9},{11,1... | collective-permute-start | bytes 73736 | tf_op jit(solution)/shard_map/ppermute | solution.py:20
  25.1 5.7 %collective-permute-start.5 = (f32[2,1,6144]{2,1,0:T(1,128)S(1)}, f32[2,1,6144]{2,1,0:T(1,128)S(1)}, u32[]{:S(2)}, u32[]{:S(2)}) collective-permute-start(f32[2,1,6144]{2,1,0:T(1,128)S(1)} %get-tuple-element.121), channel_id=1, source_target_pairs={{1,0},{2,1},{3,2},{4,3},{5,4},{6,5},{7,6},{8,7},{9,8},{10,9},{11,1... | collective-permute-start | bytes 147464 | tf_op jit(solution)/shard_map/ppermute | solution.py:20
  27.0 4.8 %collective-permute-start.4 = (f32[2,1,6144]{2,1,0:T(1,128)S(1)}, f32[2,1,6144]{2,1,0:T(1,128)S(1)}, u32[]{:S(2)}, u32[]{:S(2)}) collective-permute-start(f32[2,1,6144]{2,1,0:T(1,128)S(1)} %get-tuple-element.122), channel_id=1, source_target_pairs={{0,1},{1,2},{2,3},{3,4},{4,5},{5,6},{6,7},{7,8},{8,9},{9,10},{10,1... | collective-permute-start | bytes 147464 | tf_op jit(solution)/shard_map/ppermute | solution.py:19
  33.2 6.3 %collective-permute-start.7 = (f32[2,1,6144]{2,1,0:T(1,128)S(1)}, f32[2,1,6144]{2,1,0:T(1,128)S(1)}, u32[]{:S(2)}, u32[]{:S(2)}) collective-permute-start(f32[2,1,6144]{2,1,0:T(1,128)S(1)} %get-tuple-element.117), channel_id=1, source_target_pairs={{1,0},{2,1},{3,2},{4,3},{5,4},{6,5},{7,6},{8,7},{9,8},{10,9},{11,1... | collective-permute-start | bytes 147464 | tf_op jit(solution)/shard_map/ppermute | solution.py:20
  35.2 5.4 %collective-permute-start.6 = (f32[2,1,6144]{2,1,0:T(1,128)S(1)}, f32[2,1,6144]{2,1,0:T(1,128)S(1)}, u32[]{:S(2)}, u32[]{:S(2)}) collective-permute-start(f32[2,1,6144]{2,1,0:T(1,128)S(1)} %get-tuple-element.118), channel_id=1, source_target_pairs={{0,1},{1,2},{2,3},{3,4},{4,5},{5,6},{6,7},{7,8},{8,9},{9,10},{10,1... | collective-permute-start | bytes 147464 | tf_op jit(solution)/shard_map/ppermute | solution.py:19
  41.9 11.1 %copy-start.4 = (f32[1,2,8,6144]{3,2,1,0:T(8,128)S(1)}, f32[1,2,8,6144]{3,2,1,0:T(8,128)}, u32[]{:S(2)}) copy-start(f32[1,2,8,6144]{3,2,1,0:T(8,128)} %param.6) | copy-start | bytes 1179652
  42.0 6.4 %collective-permute-start.8 = (f32[2,1,6144]{2,1,0:T(1,128)S(1)}, f32[2,1,6144]{2,1,0:T(1,128)S(1)}, u32[]{:S(2)}, u32[]{:S(2)}) collective-permute-start(f32[2,1,6144]{2,1,0:T(1,128)S(1)} %get-tuple-element.113), channel_id=1, source_target_pairs={{0,1},{1,2},{2,3},{3,4},{4,5},{5,6},{6,7},{7,8},{8,9},{9,10},{10,1... | collective-permute-start | bytes 147464 | tf_op jit(solution)/shard_map/ppermute | solution.py:19
  46.4 5.4 %collective-permute-start.9 = (f32[2,1,6144]{2,1,0:T(1,128)S(1)}, f32[2,1,6144]{2,1,0:T(1,128)S(1)}, u32[]{:S(2)}, u32[]{:S(2)}) collective-permute-start(f32[2,1,6144]{2,1,0:T(1,128)S(1)} %get-tuple-element.114), channel_id=1, source_target_pairs={{1,0},{2,1},{3,2},{4,3},{5,4},{6,5},{7,6},{8,7},{9,8},{10,9},{11,1... | collective-permute-start | bytes 147464 | tf_op jit(solution)/shard_map/ppermute | solution.py:20
  52.1 1.3 copy-start
  54.9 4.3 %collective-permute-start.10 = (f32[2,1,6144]{2,1,0:T(1,128)S(1)}, f32[2,1,6144]{2,1,0:T(1,128)S(1)}, u32[]{:S(2)}, u32[]{:S(2)}) collective-permute-start(f32[2,1,6144]{2,1,0:T(1,128)S(1)} %get-tuple-element.92), channel_id=1, source_target_pairs={{0,1},{1,2},{2,3},{3,4},{4,5},{5,6},{6,7},{7,8},{8,9},{9,10},{10,1... | collective-permute-start | bytes 147464 | tf_op jit(solution)/shard_map/ppermute | solution.py:19
  56.9 5.7 %collective-permute-start.11 = (f32[2,1,6144]{2,1,0:T(1,128)S(1)}, f32[2,1,6144]{2,1,0:T(1,128)S(1)}, u32[]{:S(2)}, u32[]{:S(2)}) collective-permute-start(f32[2,1,6144]{2,1,0:T(1,128)S(1)} %get-tuple-element.93), channel_id=1, source_target_pairs={{1,0},{2,1},{3,2},{4,3},{5,4},{6,5},{7,6},{8,7},{9,8},{10,9},{11,1... | collective-permute-start | bytes 147464 | tf_op jit(solution)/shard_map/ppermute | solution.py:20
  64.5 4.3 %collective-permute-start.12 = (f32[2,1,6144]{2,1,0:T(1,128)S(1)}, f32[2,1,6144]{2,1,0:T(1,128)S(1)}, u32[]{:S(2)}, u32[]{:S(2)}) collective-permute-start(f32[2,1,6144]{2,1,0:T(1,128)S(1)} %get-tuple-element.90), channel_id=1, source_target_pairs={{0,1},{1,2},{2,3},{3,4},{4,5},{5,6},{6,7},{7,8},{8,9},{9,10},{10,1... | collective-permute-start | bytes 147464 | tf_op jit(solution)/shard_map/ppermute | solution.py:19
  66.5 8.5 %collective-permute-start.13 = (f32[2,1,6144]{2,1,0:T(1,128)S(1)}, f32[2,1,6144]{2,1,0:T(1,128)S(1)}, u32[]{:S(2)}, u32[]{:S(2)}) collective-permute-start(f32[2,1,6144]{2,1,0:T(1,128)S(1)} %get-tuple-element.91), channel_id=1, source_target_pairs={{1,0},{2,1},{3,2},{4,3},{5,4},{6,5},{7,6},{8,7},{9,8},{10,9},{11,1... | collective-permute-start | bytes 147464 | tf_op jit(solution)/shard_map/ppermute | solution.py:20
  76.9 4.5 %collective-permute-start.14 = (f32[2,1,6144]{2,1,0:T(1,128)S(1)}, f32[2,1,6144]{2,1,0:T(1,128)S(1)}, u32[]{:S(2)}, u32[]{:S(2)}) collective-permute-start(f32[2,1,6144]{2,1,0:T(1,128)S(1)} %get-tuple-element.88), channel_id=1, source_target_pairs={{0,1},{1,2},{2,3},{3,4},{4,5},{5,6},{6,7},{7,8},{8,9},{9,10},{10,1... | collective-permute-start | bytes 147464 | tf_op jit(solution)/shard_map/ppermute | solution.py:19
  79.3 9.8 %collective-permute-start.15 = (f32[2,1,6144]{2,1,0:T(1,128)S(1)}, f32[2,1,6144]{2,1,0:T(1,128)S(1)}, u32[]{:S(2)}, u32[]{:S(2)}) collective-permute-start(f32[2,1,6144]{2,1,0:T(1,128)S(1)} %get-tuple-element.89), channel_id=1, source_target_pairs={{1,0},{2,1},{3,2},{4,3},{5,4},{6,5},{7,6},{8,7},{9,8},{10,9},{11,1... | collective-permute-start | bytes 147464 | tf_op jit(solution)/shard_map/ppermute | solution.py:20
  91.8 4.7 %collective-permute-start.16 = (f32[1,6144]{1,0:T(1,128)S(1)}, f32[1,6144]{1,0:T(1,128)S(1)}, u32[]{:S(2)}, u32[]{:S(2)}) collective-permute-start(f32[1,6144]{1,0:T(1,128)S(1)} %add_add_fusion.4), channel_id=1, source_target_pairs={{0,1},{1,2},{2,3},{3,4},{4,5},{5,6},{6,7},{7,8},{8,9},{9,10},{10,1... | collective-permute-start | bytes 73736 | tf_op jit(solution)/shard_map/ppermute | solution.py:19
  93.7 6.4 %collective-permute-start.17 = (f32[1,6144]{1,0:T(1,128)S(1)}, f32[1,6144]{1,0:T(1,128)S(1)}, u32[]{:S(2)}, u32[]{:S(2)}) collective-permute-start(f32[1,6144]{1,0:T(1,128)S(1)} %add_add_fusion.3), channel_id=1, source_target_pairs={{1,0},{2,1},{3,2},{4,3},{5,4},{6,5},{7,6},{8,7},{9,8},{10,9},{11,1... | collective-permute-start | bytes 73736 | tf_op jit(solution)/shard_map/ppermute | solution.py:20
Sparse Core Ops, SparseCore 0:
  101.1 69.0 all-gather.2
